TPU v7x, 32 devices: a whole 2x2x4 slice. The times are simulated.
32 devices in a mesh: parts: 2 (over x), tok: 8 (over z, y), sub: 2 (over core).
Axes of the slice: x: 2, y: 2, z: 4, core: 2. Of those that a mesh axis runs over, the one named last changes fastest.
Arguments:
- video: bfloat16 [16, 48, 16, 768], P('parts', None, ('tok', 'sub')), parts along dimension 0, may hold values from -6 to 6
- norm_gain: float32 [3, 768], replicated, may hold values from 0.1 to 1.9
- qkv_weight: bfloat16 [3, 3, 768, 768], P(None, None, None, 'sub'), may hold values from -0.21875 to 0.21875
- out_weight: bfloat16 [3, 768, 768], P(None, 'sub'), may hold values from -0.21875 to 0.21875
Outputs:
- refined: bfloat16 [16, 48, 16, 768], P('parts', None, ('tok', 'sub')), parts along dimension 0
There are 2 independent parts, one for each index of `parts`. A program takes and returns all parts, laid end to end along the dimension named above; an argument that names none is the same for every part. Nothing has to cross between parts.
All inputs are finite; a program needn't handle non-finite values.
Results may differ from a plain program's by a relative error of at most 0.014.
Values may be sent and summed in bfloat16 or wider, within the bound.
No kernel may reach another device: no remote copies, remote signals or barrier semaphores. Data moves between devices by JAX's collectives and lax.ppermute only.
A program may use at most 64 MiB of HBM per device.

v0:
```python
import math
import jax
import jax.numpy as jnp
from jax import lax
from jax.sharding import PartitionSpec as P

HEAD_DIM = 64
EPSILON = 1e-06


def normalize(tokens, gain):
    values = tokens.astype(jnp.float32)
    scale = lax.rsqrt(jnp.mean(values * values, axis=-1, keepdims=True) + EPSILON)
    return (values * scale * gain).astype(jnp.bfloat16)


def head_norm(values, shape):
    split = values.reshape(shape + (values.shape[-1] // HEAD_DIM, HEAD_DIM))
    scale = lax.rsqrt(jnp.mean(split * split, axis=-1, keepdims=True) + EPSILON)
    return (split * scale).astype(jnp.bfloat16)


def attend(query, key, value, shape):
    query_n = head_norm(query, shape)
    key_n = head_norm(key, shape)
    value_b = value.reshape(query_n.shape).astype(jnp.bfloat16)
    scores = jnp.einsum(
        "plqhe,pmqhe->pqhlm", query_n, key_n, preferred_element_type=jnp.float32
    ) / math.sqrt(HEAD_DIM)
    expo = jnp.exp(scores)
    probs = (expo / jnp.sum(expo, axis=-1, keepdims=True)).astype(jnp.bfloat16)
    mixed = jnp.einsum("pqhlm,pmqhe->plqhe", probs, value_b, preferred_element_type=jnp.float32)
    return mixed.astype(jnp.bfloat16).reshape(query.shape)


def sublayer(tokens, gain, qkv_part, out_part):
    shape = tokens.shape[:3]
    width = tokens.shape[3]
    normed = normalize(tokens, gain)
    flat = normed.reshape(-1, width)
    qkv = jnp.einsum(
        "nd,jde->jne",
        flat,
        lax.all_gather(qkv_part, "sub", axis=2, tiled=True),
        preferred_element_type=jnp.float32,
    )
    mixed = attend(qkv[0], qkv[1], qkv[2], shape)
    update = jnp.dot(
        mixed,
        lax.all_gather(out_part, "sub", axis=0, tiled=True),
        preferred_element_type=jnp.float32,
    ).reshape(tokens.shape)
    return (tokens.astype(jnp.float32) + update).astype(jnp.bfloat16)


def body(video, norm_gain, qkv_weight, out_weight):
    frames, rows, cols, width = video.shape
    state = sublayer(
        video.reshape(1, frames, rows * cols, width), norm_gain[0], qkv_weight[0], out_weight[0]
    ).reshape(video.shape)
    outer = lax.axis_size("tok")
    inner = lax.axis_size("sub")
    devices = outer * inner
    blocks = frames * rows // devices
    stacked = state.reshape(blocks, devices, cols, width)
    items = lax.all_to_all(stacked, ("tok", "sub"), split_axis=1, concat_axis=2, tiled=True)
    lines = items.reshape(items.shape[0], -1, 1, width)
    turned = sublayer(lines, norm_gain[1], qkv_weight[1], out_weight[1]).reshape(items.shape)
    returned = lax.all_to_all(turned, ("tok", "sub"), split_axis=2, concat_axis=1, tiled=True)
    state = returned.reshape(video.shape)
    return sublayer(state, norm_gain[2], qkv_weight[2], out_weight[2])


def solution(mesh):
    in_specs = (
        P("parts", None, ("tok", "sub"), None),
        P(),
        P(None, None, None, "sub"),
        P(None, "sub", None),
    )
    out_specs = P("parts", None, ("tok", "sub"), None)
    return jax.shard_map(body, mesh=mesh, in_specs=in_specs, out_specs=out_specs, check_vma=False)
```

profile of v0, /device:TPU:0, one launch (start us, length us, event | category | flops | bytes accessed | tf_op | source)
XLA Modules:
  0.0 176.2 jit_solution(2934585236718387457)
XLA Ops:
  6.5 5.1 %fusion.56 = (bf16[1,3,768,384]{3,2,1,0:T(8,128)(2,1)}, bf16[1,3,768,384]{3,2,1,0:T(8,128)(2,1)}, bf16[1,3,768,384]{3,2,1,0:T(8,128)(2,1)}) fusion(bf16[3,3,768,384]{3,2,1,0:T(8,128)(2,1)} %param.6), kind=kLoop, calls=%fused_computation.98 | loop fusion | bytes 10616832 | tf_op jit(solution)/shard_map/slice | solution.py:71
  11.7 1.4 copy-done.9
  13.1 1.2 fusion.57
  14.4 0.7 all-gather.17.cloned.1.call-update
  15.1 0.5 all-gather.19.cloned.1.call-update
  16.3 10.8 %all-gather.13.cloned.1.call-done = bf16[1,3,768,768]{3,2,1,0:T(8,128)(2,1)} async-done(((bf16[1,3,768,384]{3,2,1,0:T(8,128)(2,1)}), bf16[1,3,768,768]{3,2,1,0:T(8,128)(2,1)}) %all-gather.13.cloned.1.call-update) | async-done | bytes 3538960 | tf_op jit(solution)/shard_map/all_gather | solution.py:44
  27.1 3.5 %fusion.9 = f32[3,384,768]{2,1,0:T(8,128)S(1)} fusion(bf16[1,3,768,768]{3,2,1,0:T(8,128)(2,1)} %all-gather.13.cloned.1.call-done, bf16[384,768]{1,0:T(8,128)(2,1)S(1)} %fusion.34), kind=kOutput, calls=%fused_computation.21 | convolution fusion | flops 1358954496 | bytes 7667712 | tf_op jit(solution)/shard_map/nd,jde->jne/dot_general | solution.py:41
  30.7 2.3 %slice_multiply_fusion.5 = (f32[1,384,768]{2,1,0:T(8,128)}, f32[1,384,768]{2,1,0:T(8,128)}, f32[1,384,768]{2,1,0:T(8,128)}, f32[1,384,768]{2,1,0:T(8,128)}) fusion(f32[3,384,768]{2,1,0:T(8,128)S(1)} %fusion.9), kind=kLoop, calls=%fused_computation.97 | loop fusion | flops 589824 | bytes 7077888 | tf_op jit(solution)/shard_map/mul | solution.py:19
  33.0 0.9 slice.98
  33.9 1.8 %mul.281 = f32[8,48,12,64]{3,2,1,0:T(8,128)S(1)} reshape(f32[1,384,768]{2,1,0:T(8,128)} %get-tuple-element.20) | data formatting | bytes 2359296 | tf_op jit(solution)/shard_map/mul | solution.py:19
  35.7 0.9 reduce_sum.110
  36.6 1.8 %mul.277 = f32[8,48,12,64]{3,2,1,0:T(8,128)S(1)} reshape(f32[1,384,768]{2,1,0:T(8,128)} %get-tuple-element.19) | data formatting | bytes 2359296 | tf_op jit(solution)/shard_map/mul | solution.py:19
  38.4 0.9 reduce_sum.109
  39.3 0.7 add_rsqrt_fusion.5
  40.0 1.8 %reshape_squeeze.21 = f32[8,48,12,64]{3,2,1,0:T(8,128)S(1)} reshape(f32[1,384,768]{2,1,0:T(8,128)} %get-tuple-element.22) | data formatting | bytes 2359296 | tf_op jit(solution)/shard_map/reshape;squeeze | solution.py:18
  41.8 3.1 %reshape_squeeze.22 = f32[8,48,12,64]{3,2,1,0:T(8,128)} reshape(f32[1,384,768]{2,1,0:T(8,128)} %get-tuple-element.21) | data formatting | bytes 2359296 | tf_op jit(solution)/shard_map/reshape;squeeze | solution.py:18
  44.9 2.8 %convert_element_type.199 = bf16[8,48,12,64]{3,2,1,0:T(8,128)(2,1)} reshape(bf16[1,384,768]{2,1,0:T(8,128)(2,1)} %slice.98) | data formatting | bytes 1179648 | tf_op jit(solution)/shard_map/convert_element_type | solution.py:26
  47.8 4.0 %multiply_convert_fusion.4 = (bf16[8,48,12,64]{3,2,1,0:T(8,128)(2,1)S(1)}, bf16[8,48,12,64]{3,2,1,0:T(8,128)(2,1)S(1)}) fusion(f32[8,48,12,64]{3,2,1,0:T(8,128)} %reshape_squeeze.22, f32[8,48,12]{2,1,0:T(8,128)S(1)} %add_rsqrt_fusion.4, f32[8,48,12,64]{3,2,1,0:T(8,128)S(1)} %reshape_squeeze.21, f32[8,48,12]{2,1,0:T(8,128)S(1)} %copy-done.13), kind=kLoop, calls=%fused_computation.10 | loop fusion | flops 1179648 | bytes 3575808 | tf_op jit(solution)/shard_map/convert_element_type | solution.py:20
  51.7 2.0 %fusion.6 = (f32[48,12,8]{2,1,0:T(8,128)S(1)}, f32[48,12,8,8]{2,3,1,0:T(8,128)S(1)}) fusion(bf16[8,48,12,64]{3,2,1,0:T(8,128)(2,1)S(1)} %get-tuple-element.32, bf16[8,48,12,64]{3,2,1,0:T(8,128)(2,1)S(1)} %get-tuple-element.33), kind=kOutput, calls=%fused_computation.18 | convolution fusion | flops 4787712 | bytes 1345536 | tf_op jit(solution)/shard_map/plqhe,pmqhe->pqhlm/dot_general | solution.py:27
  53.7 1.2 fusion.18
  55.2 0.9 dot_general.45
  56.3 1.9 %fusion.21 = bf16[8,48,768]{2,1,0:T(8,128)(2,1)S(1)} fusion(bf16[8,48,768]{2,1,0:T(8,128)(2,1)S(1)} %dot_general.45, bf16[1,768,768]{2,1,0:T(8,128)(2,1)} %all-gather.15.cloned.1.call-done, bf16[8,48,1,768]{3,1,2,0:T(8,128)(2,1)S(1)} %copy-done.8), kind=kOutput, calls=%fused_computation.33 | convolution fusion | flops 453869568 | bytes 2949120 | tf_op jit(solution)/shard_map/dot_general | solution.py:48
  58.2 1.0 copy.65
  59.2 5.9 %all-to-all-start = ((bf16[24,16,1,768]{3,0,2,1:T(8,128)(2,1)}), bf16[24,16,1,768]{3,0,2,1:T(8,128)(2,1)S(1)}, u32[]{:S(2)}, u32[]{:S(2)}) async-start(bf16[24,16,1,768]{3,0,2,1:T(8,128)(2,1)} %copy.65), calls=%async_computation | async-start | bytes 1179648 | tf_op jit(solution)/shard_map/all_to_all | solution.py:66
  65.7 14.8 %all-to-all-done = bf16[24,16,1,768]{3,0,2,1:T(8,128)(2,1)S(1)} async-done(((bf16[24,16,1,768]{3,0,2,1:T(8,128)(2,1)}), bf16[24,16,1,768]{3,0,2,1:T(8,128)(2,1)S(1)}, u32[]{:S(2)}, u32[]{:S(2)}) %all-to-all-start) | async-done | bytes 589856 | tf_op jit(solution)/shard_map/all_to_all | solution.py:66
  81.3 3.5 %fusion.12 = f32[3,384,768]{2,1,0:T(8,128)S(1)} fusion(bf16[1,3,768,768]{3,2,1,0:T(8,128)(2,1)} %all-gather.17.cloned.1.call-done, bf16[384,768]{1,0:T(8,128)(2,1)S(1)} %fusion.31), kind=kOutput, calls=%fused_computation.22 | convolution fusion | flops 1358954496 | bytes 7667712 | tf_op jit(solution)/shard_map/nd,jde->jne/dot_general | solution.py:41
  84.8 0.9 slice.97
  85.7 2.4 %slice_multiply_fusion.3 = (f32[1,384,768]{2,1,0:T(8,128)}, f32[1,384,768]{2,1,0:T(8,128)}, f32[1,384,768]{2,1,0:T(8,128)}, f32[1,384,768]{2,1,0:T(8,128)}) fusion(f32[3,384,768]{2,1,0:T(8,128)S(1)} %fusion.12), kind=kLoop, calls=%fused_computation.95 | loop fusion | flops 589824 | bytes 7077888 | tf_op jit(solution)/shard_map/mul | solution.py:19
  88.1 1.8 %mul.291 = f32[24,16,12,64]{3,2,1,0:T(8,128)S(1)} reshape(f32[1,384,768]{2,1,0:T(8,128)} %get-tuple-element.15) | data formatting | bytes 2359296 | tf_op jit(solution)/shard_map/mul | solution.py:19
  89.9 0.9 reduce_sum.113
  90.8 1.8 %reshape_squeeze.23 = f32[24,16,12,64]{3,2,1,0:T(8,128)S(1)} reshape(f32[1,384,768]{2,1,0:T(8,128)} %get-tuple-element.18) | data formatting | bytes 2359296 | tf_op jit(solution)/shard_map/reshape;squeeze | solution.py:18
  92.6 3.1 %mul.295 = f32[24,16,12,64]{3,2,1,0:T(8,128)} reshape(f32[1,384,768]{2,1,0:T(8,128)} %get-tuple-element.16) | data formatting | bytes 2359296 | tf_op jit(solution)/shard_map/mul | solution.py:19
  95.7 2.8 %reduce_sum.114 = f32[24,16,12]{2,1,0:T(8,128)S(1)} reduce(f32[24,16,12,64]{3,2,1,0:T(8,128)} %mul.295, f32[]{:T(128)} %constant.12.clone.1), dimensions={3}, to_apply=%region_6.0 | reduce | flops 290304 | bytes 1198084 | tf_op jit(solution)/shard_map/reduce_sum | solution.py:19
  98.5 3.1 %reshape_squeeze.24 = f32[24,16,12,64]{3,2,1,0:T(8,128)} reshape(f32[1,384,768]{2,1,0:T(8,128)} %get-tuple-element.17) | data formatting | bytes 2359296 | tf_op jit(solution)/shard_map/reshape;squeeze | solution.py:18
  101.6 2.8 %convert_element_type.213 = bf16[24,16,12,64]{3,2,1,0:T(8,128)(2,1)} reshape(bf16[1,384,768]{2,1,0:T(8,128)(2,1)} %slice.97) | data formatting | bytes 1179648 | tf_op jit(solution)/shard_map/convert_element_type | solution.py:26
  104.5 1.0 multiply_convert_fusion.3
  105.5 0.9 copy-done
  106.4 1.0 multiply_convert_fusion.2
  107.4 1.0 fusion.7
  108.8 0.8 fusion.19
  110.0 0.9 dot_general.50
  111.1 1.9 %fusion.25 = bf16[24,1,16,768]{3,2,0,1:T(8,128)(2,1)S(1)} fusion(bf16[24,16,768]{2,1,0:T(8,128)(2,1)S(1)} %dot_general.50, bf16[1,768,768]{2,1,0:T(8,128)(2,1)} %all-gather.19.cloned.1.call-done, bf16[24,16,1,768]{3,0,2,1:T(8,128)(2,1)S(1)} %copy-done.4), kind=kOutput, calls=%fused_computation.37 | convolution fusion | flops 453869568 | bytes 2949120 | tf_op jit(solution)/shard_map/dot_general | solution.py:48
  113.0 1.0 copy.72
  114.0 4.5 %all-to-all-start.1 = ((bf16[24,1,16,768]{3,0,1,2:T(8,128)(2,1)}), bf16[24,1,16,768]{3,0,1,2:T(8,128)(2,1)S(1)}, u32[]{:S(2)}, u32[]{:S(2)}) async-start(bf16[24,1,16,768]{3,0,1,2:T(8,128)(2,1)} %copy.72), calls=%async_computation.1 | async-start | bytes 1179648 | tf_op jit(solution)/shard_map/all_to_all | solution.py:69
  119.0 14.8 %all-to-all-done.1 = bf16[24,1,16,768]{3,0,1,2:T(8,128)(2,1)S(1)} async-done(((bf16[24,1,16,768]{3,0,1,2:T(8,128)(2,1)}), bf16[24,1,16,768]{3,0,1,2:T(8,128)(2,1)S(1)}, u32[]{:S(2)}, u32[]{:S(2)}) %all-to-all-start.1) | async-done | bytes 589856 | tf_op jit(solution)/shard_map/all_to_all | solution.py:69
  134.3 1.0 copy-done.1
  135.5 3.5 %fusion.15 = f32[3,384,768]{2,1,0:T(8,128)S(1)} fusion(bf16[1,3,768,768]{3,2,1,0:T(8,128)(2,1)} %all-gather.21.cloned.1.call-done, bf16[384,768]{1,0:T(8,128)(2,1)S(1)} %fusion.28), kind=kOutput, calls=%fused_computation.23 | convolution fusion | flops 1358954496 | bytes 7667712 | tf_op jit(solution)/shard_map/nd,jde->jne/dot_general | solution.py:41
  139.0 2.5 %slice_multiply_fusion.1 = (f32[1,384,768]{2,1,0:T(8,128)}, f32[1,384,768]{2,1,0:T(8,128)}, f32[1,384,768]{2,1,0:T(8,128)}, f32[1,384,768]{2,1,0:T(8,128)}) fusion(f32[3,384,768]{2,1,0:T(8,128)S(1)} %fusion.15), kind=kLoop, calls=%fused_computation.93 | loop fusion | flops 589824 | bytes 7077888 | tf_op jit(solution)/shard_map/mul | solution.py:19
  141.5 0.7 copy-done.6
  142.2 1.8 %mul.305 = f32[8,48,12,64]{3,2,1,0:T(8,128)S(1)} reshape(f32[1,384,768]{2,1,0:T(8,128)} %get-tuple-element.11) | data formatting | bytes 2359296 | tf_op jit(solution)/shard_map/mul | solution.py:19
  144.1 0.9 reduce_sum.117
  145.0 1.8 %reshape_squeeze.25 = f32[8,48,12,64]{3,2,1,0:T(8,128)S(1)} reshape(f32[1,384,768]{2,1,0:T(8,128)} %get-tuple-element.14) | data formatting | bytes 2359296 | tf_op jit(solution)/shard_map/reshape;squeeze | solution.py:18
  146.8 3.1 %mul.309 = f32[8,48,12,64]{3,2,1,0:T(8,128)} reshape(f32[1,384,768]{2,1,0:T(8,128)} %get-tuple-element.12) | data formatting | bytes 2359296 | tf_op jit(solution)/shard_map/mul | solution.py:19
  149.9 2.8 %reduce_sum.118 = f32[8,48,12]{2,1,0:T(8,128)S(1)} reduce(f32[8,48,12,64]{3,2,1,0:T(8,128)} %mul.309, f32[]{:T(128)} %constant.12.clone.1), dimensions={3}, to_apply=%region_10.0 | reduce | flops 290304 | bytes 1198084 | tf_op jit(solution)/shard_map/reduce_sum | solution.py:19
  152.7 1.9 %multiply_convert_fusion.1 = bf16[8,48,12,64]{3,2,1,0:T(8,128)(2,1)} fusion(f32[8,48,12,64]{3,2,1,0:T(8,128)S(1)} %reshape_squeeze.25, f32[8,48,12]{2,1,0:T(8,128)S(1)} %add_rsqrt_fusion.1), kind=kLoop, calls=%fused_computation.7 | loop fusion | flops 589824 | bytes 1787904 | tf_op jit(solution)/shard_map/convert_element_type | solution.py:20
  154.6 2.1 %slice.96 = bf16[1,384,768]{2,1,0:T(8,128)(2,1)} slice(f32[3,384,768]{2,1,0:T(8,128)} %copy-done.6), slice={[2:3], [0:384], [0:768]} | slice | bytes 1179648 | tf_op jit(solution)/shard_map/slice | solution.py:47
  156.7 1.8 %reshape_squeeze.26 = f32[8,48,12,64]{3,2,1,0:T(8,128)S(1)} reshape(f32[1,384,768]{2,1,0:T(8,128)} %get-tuple-element.13) | data formatting | bytes 2359296 | tf_op jit(solution)/shard_map/reshape;squeeze | solution.py:18
  158.5 2.8 %convert_element_type.227 = bf16[8,48,12,64]{3,2,1,0:T(8,128)(2,1)} reshape(bf16[1,384,768]{2,1,0:T(8,128)(2,1)} %slice.96) | data formatting | bytes 1179648 | tf_op jit(solution)/shard_map/convert_element_type | solution.py:26
  161.4 1.0 multiply_convert_fusion
  162.8 0.9 fusion.8
  163.7 0.5 copy-done.12
  164.2 0.8 fusion.20
  165.3 0.9 dot_general.55
  166.6 2.7 %fusion.24 = bf16[8,48,1,768]{3,1,2,0:T(8,128)(2,1)} fusion(f32[8,48,768]{2,1,0:T(8,128)S(1)} %bitcast.97, bf16[8,48,768]{2,1,0:T(8,128)(2,1)S(1)} %dot_general.55, bf16[1,768,768]{2,1,0:T(8,128)(2,1)} %all-gather.23.cloned.1.call-done), kind=kOutput, calls=%fused_computation.36 | convolution fusion | flops 453574656 | bytes 3538944 | tf_op jit(solution)/shard_map/dot_general | solution.py:48
  (64 shorter events, 5.9 us)
Async XLA Ops:
  6.5 20.6 %all-gather.13.cloned.1.call-start = ((), (), s32[]{:S(2)}) async-start(), calls=%async_computation.2 | async-start | bytes 5308416 | tf_op jit(solution)/shard_map/all_gather | solution.py:44
  11.6 1.5 copy-start.9
  11.6 44.5 %all-gather.15.cloned.1.call-start = ((), (), s32[]{:S(2)}) async-start(), calls=%async_computation.3 | async-start | bytes 1769472 | tf_op jit(solution)/shard_map/all_gather | solution.py:50
  14.3 1.4 copy-start.7
  14.3 66.9 %all-gather.17.cloned.1.call-start = ((), (), s32[]{:S(2)}) async-start(), calls=%async_computation.4 | async-start | bytes 5308416 | tf_op jit(solution)/shard_map/all_gather | solution.py:44
  15.1 0.9 copy-start.14
  15.1 95.9 %all-gather.19.cloned.1.call-start = ((), (), s32[]{:S(2)}) async-start(), calls=%async_computation.5 | async-start | bytes 1769472 | tf_op jit(solution)/shard_map/all_gather | solution.py:50
  44.9 2.8 %copy-start.13 = (f32[8,48,12]{2,1,0:T(8,128)S(1)}, f32[8,48,12]{2,1,0:T(8,128)}, u32[]{:S(2)}) copy-start(f32[8,48,12]{2,1,0:T(8,128)} %add_rsqrt_fusion.5) | copy-start | bytes 55300
  51.7 2.0 %copy-start.11 = (bf16[8,48,12,64]{3,2,1,0:T(8,128)(2,1)S(1)}, bf16[8,48,12,64]{3,2,1,0:T(8,128)(2,1)}, u32[]{:S(2)}) copy-start(bf16[8,48,12,64]{3,2,1,0:T(8,128)(2,1)} %convert_element_type.199) | copy-start | bytes 1769476
  55.2 1.1 copy-start.8
  59.2 21.3 %all-to-all-start = ((bf16[24,16,1,768]{3,0,2,1:T(8,128)(2,1)}), bf16[24,16,1,768]{3,0,2,1:T(8,128)(2,1)S(1)}, u32[]{:S(2)}, u32[]{:S(2)}) async-start(bf16[24,16,1,768]{3,0,2,1:T(8,128)(2,1)} %copy.65), calls=%async_computation | async-start | bytes 1179648 | tf_op jit(solution)/shard_map/all_to_all | solution.py:66
  65.1 70.4 %all-gather.21.cloned.1.call-start = ((), (), s32[]{:S(2)}) async-start(), calls=%async_computation.6 | async-start | bytes 5308416 | tf_op jit(solution)/shard_map/all_gather | solution.py:44
  80.4 0.8 copy-start.3
  104.5 1.9 %copy-start = (f32[24,16,12,64]{3,2,1,0:T(8,128)S(1)}, f32[24,16,12,64]{3,2,1,0:T(8,128)}, u32[]{:S(2)}) copy-start(f32[24,16,12,64]{3,2,1,0:T(8,128)} %reshape_squeeze.24) | copy-start | bytes 3538948
  107.4 1.4 copy-start.10
  110.0 1.1 copy-start.4
  114.0 19.9 %all-to-all-start.1 = ((bf16[24,1,16,768]{3,0,1,2:T(8,128)(2,1)}), bf16[24,1,16,768]{3,0,1,2:T(8,128)(2,1)S(1)}, u32[]{:S(2)}, u32[]{:S(2)}) async-start(bf16[24,1,16,768]{3,0,1,2:T(8,128)(2,1)} %copy.72), calls=%async_computation.1 | async-start | bytes 1179648 | tf_op jit(solution)/shard_map/all_to_all | solution.py:69
  118.4 47.8 %all-gather.23.cloned.1.call-start = ((), (), s32[]{:S(2)}) async-start(), calls=%async_computation.7 | async-start | bytes 1769472 | tf_op jit(solution)/shard_map/all_gather | solution.py:50
  134.3 1.0 copy-start.1
  139.0 3.2 %copy-start.6 = (f32[3,384,768]{2,1,0:T(8,128)}, f32[3,384,768]{2,1,0:T(8,128)S(1)}, u32[]{:S(2)}) copy-start(f32[3,384,768]{2,1,0:T(8,128)S(1)} %fusion.15) | copy-start | bytes 10616836
  161.4 1.4 copy-start.5
  162.8 1.4 copy-start.12
  165.3 1.3 copy-start.2
Sparse Core Ops, SparseCore 0:
  11.8 15.3 all-gather.12
  28.6 10.3 all-gather.14
  40.6 13.7 all-gather.16
  55.8 10.3 all-gather.18
  67.7 13.7 all-gather.20
  120.5 10.5 all-gather.22
where the time goes:
time: 177 us; the launch traced here: 176 us
  local copies, waits for them, and re-layouts  57.6 us (33%)
  waiting for transfers between devices  42.4 us (24%)
  other arithmetic  27.5 us (16%)
  matrix products  23.8 us (13%)
  between operations  14 us (8%)
  starting transfers between devices  11 us (6%)
    all_to_all x1, waiting for transfers between devices, body(): lax.all_to_all(turned, ('tok', 'sub'), split_axis=2, concat_axis=1, tiled...  14.8 us
    all_to_all x1, waiting for transfers between devices, body(): lax.all_to_all(stacked, ('tok', 'sub'), split_axis=1, concat_axis=2, tile...  14.8 us
    mul x6, local copies, waits for them, and re-layouts, head_norm(): scale = lax.rsqrt(jnp.mean(split * split, axis=-1, keepdims=True) + EPSILON)  13.5 us
    another operation x6, local copies, waits for them, and re-layouts, head_norm(): split = values.reshape(shape + (values.shape[-1] // HEAD_DIM, HEAD_DIM))  13.4 us
    all_gather x3, waiting for transfers between devices, sublayer(): lax.all_gather(qkv_part, 'sub', axis=2, tiled=True)  10.8 us
    dot_general x3, matrix products, sublayer(): jnp.einsum('nd,jde->jne', flat, lax.all_gather(qkv_part, 'sub', axis=2, t...  10.6 us
    reduce_sum x6, other arithmetic, head_norm(): scale = lax.rsqrt(jnp.mean(split * split, axis=-1, keepdims=True) + EPSILON)  9.11 us
    convert_element_type x5, other arithmetic, head_norm(): return (split * scale).astype(jnp.bfloat16)  8.72 us
  transfers between devices with their start and end apart: 8, of which 3 were waited for; matrix products, arithmetic and copies ran while one was open for 54% of the time, Pallas kernels for 0%

commit v1 on v0

--- a/solution.py
+++ b/solution.py
@@ -66,7 +66,15 @@
     items = lax.all_to_all(stacked, ("tok", "sub"), split_axis=1, concat_axis=2, tiled=True)
     lines = items.reshape(items.shape[0], -1, 1, width)
     turned = sublayer(lines, norm_gain[1], qkv_weight[1], out_weight[1]).reshape(items.shape)
-    returned = lax.all_to_all(turned, ("tok", "sub"), split_axis=2, concat_axis=1, tiled=True)
+    returned = jnp.concatenate(
+        lax.all_to_all(
+            jnp.stack(jnp.split(turned, lax.axis_size(("tok", "sub")), axis=2)),
+            ("tok", "sub"),
+            0,
+            0,
+        ),
+        axis=1,
+    )
     state = returned.reshape(video.shape)
     return sublayer(state, norm_gain[2], qkv_weight[2], out_weight[2])
 

time: 177 us -> 188 us (1.062)
  local copies, waits for them, and re-layouts: 57.6 us -> 67 us
    unnamed x30 -> x45, local copies, waits for them, and re-layouts: 6.08 us -> 14.5 us
  transfers between devices with their start and end apart: 8 -> 8, of which waited for: 3 -> 3; matrix products, arithmetic and copies ran while one was open for 54% -> 57% of each run, Pallas kernels for 0% -> 0%
where the time goes in v1:
time: 188 us; the launch traced here: 187 us
  local copies, waits for them, and re-layouts  67 us (36%)
  waiting for transfers between devices  42.3 us (22%)
  other arithmetic  28.9 us (15%)
  matrix products  23.8 us (13%)
  between operations  14 us (7%)
  starting transfers between devices  10.9 us (6%)
    all_to_all x1, waiting for transfers between devices, body(): lax.all_to_all(jnp.stack(jnp.split(turned, lax.axis_size(('tok', 'sub')),...  14.8 us
    all_to_all x1, waiting for transfers between devices, body(): lax.all_to_all(stacked, ('tok', 'sub'), split_axis=1, concat_axis=2, tile...  14.8 us
    unnamed x45, local copies, waits for them, and re-layouts  14.5 us
    mul x6, local copies, waits for them, and re-layouts, head_norm(): scale = lax.rsqrt(jnp.mean(split * split, axis=-1, keepdims=True) + EPSILON)  13.4 us
    another operation x6, local copies, waits for them, and re-layouts, head_norm(): split = values.reshape(shape + (values.shape[-1] // HEAD_DIM, HEAD_DIM))  13.4 us
    all_gather x3, waiting for transfers between devices, sublayer(): lax.all_gather(qkv_part, 'sub', axis=2, tiled=True)  10.8 us
    dot_general x3, matrix products, sublayer(): jnp.einsum('nd,jde->jne', flat, lax.all_gather(qkv_part, 'sub', axis=2, t...  10.6 us
    reduce_sum x6, other arithmetic, head_norm(): scale = lax.rsqrt(jnp.mean(split * split, axis=-1, keepdims=True) + EPSILON)  9.78 us
  transfers between devices with their start and end apart: 8, of which 3 were waited for; matrix products, arithmetic and copies ran while one was open for 57% of the time, Pallas kernels for 0%

profile of v1, /device:TPU:0, one launch (start us, length us, event | category | flops | bytes accessed | tf_op | source)
XLA Modules:
  0.0 187.1 jit_solution(112651955643421401)
XLA Ops:
  6.5 5.1 %fusion.57 = (bf16[1,3,768,384]{3,2,1,0:T(8,128)(2,1)}, bf16[1,3,768,384]{3,2,1,0:T(8,128)(2,1)}, bf16[1,3,768,384]{3,2,1,0:T(8,128)(2,1)}) fusion(bf16[3,3,768,384]{3,2,1,0:T(8,128)(2,1)} %param.6), kind=kLoop, calls=%fused_computation.115 | loop fusion | bytes 10616832 | tf_op jit(solution)/shard_map/slice | solution.py:79
  11.7 1.4 copy-done.9
  13.1 1.3 fusion.58
  14.4 0.7 all-gather.17.cloned.1.call-update
  16.3 10.8 %all-gather.13.cloned.1.call-done = bf16[1,3,768,768]{3,2,1,0:T(8,128)(2,1)} async-done(((bf16[1,3,768,384]{3,2,1,0:T(8,128)(2,1)}), bf16[1,3,768,768]{3,2,1,0:T(8,128)(2,1)}) %all-gather.13.cloned.1.call-update) | async-done | bytes 3538960 | tf_op jit(solution)/shard_map/all_gather | solution.py:44
  27.1 3.5 %fusion.9 = f32[3,384,768]{2,1,0:T(8,128)S(1)} fusion(bf16[1,3,768,768]{3,2,1,0:T(8,128)(2,1)} %all-gather.13.cloned.1.call-done, bf16[384,768]{1,0:T(8,128)(2,1)S(1)} %fusion.35), kind=kOutput, calls=%fused_computation.21 | convolution fusion | flops 1358954496 | bytes 7667712 | tf_op jit(solution)/shard_map/nd,jde->jne/dot_general | solution.py:41
  30.7 2.3 %slice_multiply_fusion.5 = (f32[1,384,768]{2,1,0:T(8,128)}, f32[1,384,768]{2,1,0:T(8,128)}, f32[1,384,768]{2,1,0:T(8,128)}, f32[1,384,768]{2,1,0:T(8,128)}) fusion(f32[3,384,768]{2,1,0:T(8,128)S(1)} %fusion.9), kind=kLoop, calls=%fused_computation.114 | loop fusion | flops 589824 | bytes 7077888 | tf_op jit(solution)/shard_map/mul | solution.py:19
  33.0 0.9 slice.98
  33.9 1.8 mul.279
  35.7 0.9 reduce_sum.110
  36.6 1.8 mul.275
  38.5 0.9 reduce_sum.109
  39.3 0.7 add_rsqrt_fusion.5
  40.0 1.8 reshape_squeeze.21
  41.9 3.1 %reshape_squeeze.22 = f32[8,48,12,64]{3,2,1,0:T(8,128)} reshape(f32[1,384,768]{2,1,0:T(8,128)} %get-tuple-element.21) | data formatting | bytes 2359296 | tf_op jit(solution)/shard_map/reshape;squeeze | solution.py:18
  44.9 2.8 %convert_element_type.201 = bf16[8,48,12,64]{3,2,1,0:T(8,128)(2,1)} reshape(bf16[1,384,768]{2,1,0:T(8,128)(2,1)} %slice.98) | data formatting | bytes 1179648 | tf_op jit(solution)/shard_map/convert_element_type | solution.py:26
  47.8 4.0 %multiply_convert_fusion.4 = (bf16[8,48,12,64]{3,2,1,0:T(8,128)(2,1)S(1)}, bf16[8,48,12,64]{3,2,1,0:T(8,128)(2,1)S(1)}) fusion(f32[8,48,12,64]{3,2,1,0:T(8,128)} %reshape_squeeze.22, f32[8,48,12]{2,1,0:T(8,128)S(1)} %add_rsqrt_fusion.4, f32[8,48,12,64]{3,2,1,0:T(8,128)S(1)} %reshape_squeeze.21, f32[8,48,12]{2,1,0:T(8,128)S(1)} %copy-done.13), kind=kLoop, calls=%fused_computation.10 | loop fusion | flops 1179648 | bytes 3575808 | tf_op jit(solution)/shard_map/convert_element_type | solution.py:20
  51.7 2.0 %fusion.6 = (f32[48,12,8]{2,1,0:T(8,128)S(1)}, f32[48,12,8,8]{2,3,1,0:T(8,128)S(1)}) fusion(bf16[8,48,12,64]{3,2,1,0:T(8,128)(2,1)S(1)} %get-tuple-element.48, bf16[8,48,12,64]{3,2,1,0:T(8,128)(2,1)S(1)} %get-tuple-element.49), kind=kOutput, calls=%fused_computation.18 | convolution fusion | flops 4787712 | bytes 1345536 | tf_op jit(solution)/shard_map/plqhe,pmqhe->pqhlm/dot_general | solution.py:27
  53.8 1.2 fusion.18
  55.3 0.9 dot_general.45
  56.3 1.9 %fusion.21 = bf16[8,48,768]{2,1,0:T(8,128)(2,1)S(1)} fusion(bf16[8,48,768]{2,1,0:T(8,128)(2,1)S(1)} %dot_general.45, bf16[1,768,768]{2,1,0:T(8,128)(2,1)} %all-gather.15.cloned.1.call-done, bf16[8,48,1,768]{3,1,2,0:T(8,128)(2,1)S(1)} %copy-done.8), kind=kOutput, calls=%fused_computation.35 | convolution fusion | flops 453869568 | bytes 2949120 | tf_op jit(solution)/shard_map/dot_general | solution.py:48
  58.2 1.0 copy.451
  59.2 5.9 %all-to-all-start = ((bf16[24,16,1,768]{3,0,2,1:T(8,128)(2,1)}), bf16[24,16,1,768]{3,0,2,1:T(8,128)(2,1)S(1)}, u32[]{:S(2)}, u32[]{:S(2)}) async-start(bf16[24,16,1,768]{3,0,2,1:T(8,128)(2,1)} %copy.451), calls=%async_computation | async-start | bytes 1179648 | tf_op jit(solution)/shard_map/all_to_all | solution.py:66
  65.7 14.8 %all-to-all-done = bf16[24,16,1,768]{3,0,2,1:T(8,128)(2,1)S(1)} async-done(((bf16[24,16,1,768]{3,0,2,1:T(8,128)(2,1)}), bf16[24,16,1,768]{3,0,2,1:T(8,128)(2,1)S(1)}, u32[]{:S(2)}, u32[]{:S(2)}) %all-to-all-start) | async-done | bytes 589856 | tf_op jit(solution)/shard_map/all_to_all | solution.py:66
  81.3 3.5 %fusion.12 = f32[3,384,768]{2,1,0:T(8,128)S(1)} fusion(bf16[1,3,768,768]{3,2,1,0:T(8,128)(2,1)} %all-gather.17.cloned.1.call-done, bf16[384,768]{1,0:T(8,128)(2,1)S(1)} %fusion.32), kind=kOutput, calls=%fused_computation.22 | convolution fusion | flops 1358954496 | bytes 7667712 | tf_op jit(solution)/shard_map/nd,jde->jne/dot_general | solution.py:41
  84.8 2.4 %slice_multiply_fusion.3 = (f32[1,384,768]{2,1,0:T(8,128)}, f32[1,384,768]{2,1,0:T(8,128)}, f32[1,384,768]{2,1,0:T(8,128)}, f32[1,384,768]{2,1,0:T(8,128)}) fusion(f32[3,384,768]{2,1,0:T(8,128)S(1)} %fusion.12), kind=kLoop, calls=%fused_computation.112 | loop fusion | flops 589824 | bytes 7077888 | tf_op jit(solution)/shard_map/mul | solution.py:19
  87.2 0.9 slice.97
  88.1 1.8 mul.289
  89.9 0.9 reduce_sum.113
  90.8 1.8 reshape_squeeze.23
  92.7 3.1 %mul.293 = f32[24,16,12,64]{3,2,1,0:T(8,128)} reshape(f32[1,384,768]{2,1,0:T(8,128)} %get-tuple-element.16) | data formatting | bytes 2359296 | tf_op jit(solution)/shard_map/mul | solution.py:19
  95.8 3.5 %reduce_sum.114 = f32[24,16,12]{2,1,0:T(8,128)} reduce(f32[24,16,12,64]{3,2,1,0:T(8,128)} %mul.293, f32[]{:T(128)} %constant.12.clone.1), dimensions={3}, to_apply=%region_6.0 | reduce | flops 290304 | bytes 1198084 | tf_op jit(solution)/shard_map/reduce_sum | solution.py:19
  99.2 1.0 add_rsqrt_fusion.2
  100.2 3.1 %reshape_squeeze.24 = f32[24,16,12,64]{3,2,1,0:T(8,128)} reshape(f32[1,384,768]{2,1,0:T(8,128)} %get-tuple-element.17) | data formatting | bytes 2359296 | tf_op jit(solution)/shard_map/reshape;squeeze | solution.py:18
  103.3 2.8 %convert_element_type.215 = bf16[24,16,12,64]{3,2,1,0:T(8,128)(2,1)} reshape(bf16[1,384,768]{2,1,0:T(8,128)(2,1)} %slice.97) | data formatting | bytes 1179648 | tf_op jit(solution)/shard_map/convert_element_type | solution.py:26
  106.1 1.0 multiply_convert_fusion.3
  107.1 0.9 copy-done
  108.0 1.0 multiply_convert_fusion.2
  109.0 1.0 fusion.7
  110.4 0.8 fusion.19
  111.6 0.9 dot_general.50
  112.7 1.9 %fusion.25 = bf16[24,1,16,768]{3,2,0,1:T(8,128)(2,1)S(1)} fusion(bf16[24,16,768]{2,1,0:T(8,128)(2,1)S(1)} %dot_general.50, bf16[1,768,768]{2,1,0:T(8,128)(2,1)} %all-gather.19.cloned.1.call-done, bf16[24,16,1,768]{3,0,2,1:T(8,128)(2,1)S(1)} %copy-done.4), kind=kOutput, calls=%fused_computation.39 | convolution fusion | flops 453869568 | bytes 2949120 | tf_op jit(solution)/shard_map/dot_general | solution.py:48
  114.6 0.9 fusion.59
  115.5 0.6 bitcast_dynamic-update-slice_fusion.15
  116.8 0.6 bitcast_dynamic-update-slice_fusion.13
  125.5 4.5 %all-to-all-start.1 = ((bf16[16,24,1,1,768]{4,1,3,2,0:T(8,128)(2,1)}), bf16[16,24,1,1,768]{4,1,3,2,0:T(8,128)(2,1)S(1)}, u32[]{:S(2)}, u32[]{:S(2)}) async-start(bf16[16,24,1,1,768]{4,1,3,2,0:T(8,128)(2,1)} %bitcast_dynamic-update-slice_fusion), calls=%async_computation.1 | async-start | bytes 1179648 | tf_op jit(solution)/shard_map/all_to_all | solution.py:70
  130.5 14.8 %all-to-all-done.1 = bf16[16,24,1,1,768]{4,1,3,2,0:T(8,128)(2,1)S(1)} async-done(((bf16[16,24,1,1,768]{4,1,3,2,0:T(8,128)(2,1)}), bf16[16,24,1,1,768]{4,1,3,2,0:T(8,128)(2,1)S(1)}, u32[]{:S(2)}, u32[]{:S(2)}) %all-to-all-start.1) | async-done | bytes 589856 | tf_op jit(solution)/shard_map/all_to_all | solution.py:70
  146.4 3.5 %fusion.15 = f32[3,384,768]{2,1,0:T(8,128)S(1)} fusion(bf16[1,3,768,768]{3,2,1,0:T(8,128)(2,1)} %all-gather.21.cloned.1.call-done, bf16[384,768]{1,0:T(8,128)(2,1)S(1)} %fusion.29), kind=kOutput, calls=%fused_computation.23 | convolution fusion | flops 1358954496 | bytes 7667712 | tf_op jit(solution)/shard_map/nd,jde->jne/dot_general | solution.py:41
  150.0 2.5 %slice_multiply_fusion.1 = (f32[1,384,768]{2,1,0:T(8,128)}, f32[1,384,768]{2,1,0:T(8,128)}, f32[1,384,768]{2,1,0:T(8,128)}, f32[1,384,768]{2,1,0:T(8,128)}) fusion(f32[3,384,768]{2,1,0:T(8,128)S(1)} %fusion.15), kind=kLoop, calls=%fused_computation.110 | loop fusion | flops 589824 | bytes 7077888 | tf_op jit(solution)/shard_map/mul | solution.py:19
  152.4 0.7 copy-done.6
  153.2 1.8 mul.303
  155.0 0.9 reduce_sum.117
  155.9 1.8 reshape_squeeze.25
  157.7 3.1 %mul.307 = f32[8,48,12,64]{3,2,1,0:T(8,128)} reshape(f32[1,384,768]{2,1,0:T(8,128)} %get-tuple-element.12) | data formatting | bytes 2359296 | tf_op jit(solution)/shard_map/mul | solution.py:19
  160.8 2.8 %reduce_sum.118 = f32[8,48,12]{2,1,0:T(8,128)S(1)} reduce(f32[8,48,12,64]{3,2,1,0:T(8,128)} %mul.307, f32[]{:T(128)} %constant.12.clone.1), dimensions={3}, to_apply=%region_10.0 | reduce | flops 290304 | bytes 1198084 | tf_op jit(solution)/shard_map/reduce_sum | solution.py:19
  163.6 1.9 multiply_convert_fusion.1
  165.5 2.1 %slice.96 = bf16[1,384,768]{2,1,0:T(8,128)(2,1)} slice(f32[3,384,768]{2,1,0:T(8,128)} %copy-done.6), slice={[2:3], [0:384], [0:768]} | slice | bytes 1179648 | tf_op jit(solution)/shard_map/slice | solution.py:47
  167.6 1.8 reshape_squeeze.26
  169.5 2.8 %convert_element_type.230 = bf16[8,48,12,64]{3,2,1,0:T(8,128)(2,1)} reshape(bf16[1,384,768]{2,1,0:T(8,128)(2,1)} %slice.96) | data formatting | bytes 1179648 | tf_op jit(solution)/shard_map/convert_element_type | solution.py:26
  172.3 1.0 multiply_convert_fusion
  173.7 0.9 fusion.8
  175.1 0.8 fusion.20
  176.2 0.9 dot_general.55
  177.5 2.7 %fusion.24 = bf16[8,48,1,768]{3,1,2,0:T(8,128)(2,1)} fusion(f32[8,48,768]{2,1,0:T(8,128)S(1)} %bitcast.133, bf16[8,48,768]{2,1,0:T(8,128)(2,1)S(1)} %dot_general.55, bf16[1,768,768]{2,1,0:T(8,128)(2,1)} %all-gather.23.cloned.1.call-done), kind=kOutput, calls=%fused_computation.38 | convolution fusion | flops 453574656 | bytes 3538944 | tf_op jit(solution)/shard_map/dot_general | solution.py:48
  (82 shorter events, 16.0 us)
Async XLA Ops:
  6.5 20.6 %all-gather.13.cloned.1.call-start = ((), (), s32[]{:S(2)}) async-start(), calls=%async_computation.2 | async-start | bytes 5308416 | tf_op jit(solution)/shard_map/all_gather | solution.py:44
  11.6 1.5 copy-start.9
  11.6 44.5 %all-gather.15.cloned.1.call-start = ((), (), s32[]{:S(2)}) async-start(), calls=%async_computation.3 | async-start | bytes 1769472 | tf_op jit(solution)/shard_map/all_gather | solution.py:50
  14.4 1.4 copy-start.7
  14.4 66.9 %all-gather.17.cloned.1.call-start = ((), (), s32[]{:S(2)}) async-start(), calls=%async_computation.4 | async-start | bytes 5308416 | tf_op jit(solution)/shard_map/all_gather | solution.py:44
  15.1 0.9 copy-start.14
  15.1 97.4 %all-gather.19.cloned.1.call-start = ((), (), s32[]{:S(2)}) async-start(), calls=%async_computation.5 | async-start | bytes 1769472 | tf_op jit(solution)/shard_map/all_gather | solution.py:50
  44.9 2.8 %copy-start.13 = (f32[8,48,12]{2,1,0:T(8,128)S(1)}, f32[8,48,12]{2,1,0:T(8,128)}, u32[]{:S(2)}) copy-start(f32[8,48,12]{2,1,0:T(8,128)} %add_rsqrt_fusion.5) | copy-start | bytes 55300
  51.7 2.0 %copy-start.10 = (bf16[8,48,12,64]{3,2,1,0:T(8,128)(2,1)S(1)}, bf16[8,48,12,64]{3,2,1,0:T(8,128)(2,1)}, u32[]{:S(2)}) copy-start(bf16[8,48,12,64]{3,2,1,0:T(8,128)(2,1)} %convert_element_type.201) | copy-start | bytes 1769476
  55.2 1.1 copy-start.8
  59.2 21.3 %all-to-all-start = ((bf16[24,16,1,768]{3,0,2,1:T(8,128)(2,1)}), bf16[24,16,1,768]{3,0,2,1:T(8,128)(2,1)S(1)}, u32[]{:S(2)}, u32[]{:S(2)}) async-start(bf16[24,16,1,768]{3,0,2,1:T(8,128)(2,1)} %copy.451), calls=%async_computation | async-start | bytes 1179648 | tf_op jit(solution)/shard_map/all_to_all | solution.py:66
  65.1 81.3 %all-gather.21.cloned.1.call-start = ((), (), s32[]{:S(2)}) async-start(), calls=%async_computation.6 | async-start | bytes 5308416 | tf_op jit(solution)/shard_map/all_gather | solution.py:44
  80.5 0.8 copy-start.3
  106.1 1.9 %copy-start = (f32[24,16,12,64]{3,2,1,0:T(8,128)S(1)}, f32[24,16,12,64]{3,2,1,0:T(8,128)}, u32[]{:S(2)}) copy-start(f32[24,16,12,64]{3,2,1,0:T(8,128)} %reshape_squeeze.24) | copy-start | bytes 3538948
  109.0 1.4 copy-start.11
  111.6 1.1 copy-start.4
  125.5 19.8 %all-to-all-start.1 = ((bf16[16,24,1,1,768]{4,1,3,2,0:T(8,128)(2,1)}), bf16[16,24,1,1,768]{4,1,3,2,0:T(8,128)(2,1)S(1)}, u32[]{:S(2)}, u32[]{:S(2)}) async-start(bf16[16,24,1,1,768]{4,1,3,2,0:T(8,128)(2,1)} %bitcast_dynamic-update-slice_fusion), calls=%async_computation.1 | async-start | bytes 1179648 | tf_op jit(solution)/shard_map/all_to_all | solution.py:70
  130.0 47.2 %all-gather.23.cloned.1.call-start = ((), (), s32[]{:S(2)}) async-start(), calls=%async_computation.7 | async-start | bytes 1769472 | tf_op jit(solution)/shard_map/all_gather | solution.py:50
  145.8 4.1 %copy-start.1 = (f32[24,16,1,1,768]{4,1,0,3,2:T(8,128)}, f32[24,16,1,1,768]{4,1,0,3,2:T(8,128)S(1)}, u32[]{:S(2)}) copy-start(f32[24,16,1,1,768]{4,1,0,3,2:T(8,128)S(1)} %copy.458) | copy-start | bytes 3538948
  149.9 3.2 %copy-start.6 = (f32[3,384,768]{2,1,0:T(8,128)}, f32[3,384,768]{2,1,0:T(8,128)S(1)}, u32[]{:S(2)}) copy-start(f32[3,384,768]{2,1,0:T(8,128)S(1)} %fusion.15) | copy-start | bytes 10616836
  172.3 1.4 copy-start.5
  173.7 1.4 copy-start.12
  176.2 1.3 copy-start.2
Sparse Core Ops, SparseCore 0:
  11.8 15.3 all-gather.12
  28.7 10.3 all-gather.14
  40.6 13.7 all-gather.16
  55.8 10.3 all-gather.18
  67.7 13.7 all-gather.20
  132.0 10.5 all-gather.22
